TPU v7x, 32 devices: a whole 2x2x4 slice. The times are simulated.
32 devices in a mesh: grp: 4 (over y, x), fsdp: 8 (over z, core).
Axes of the slice: x: 2, y: 2, z: 4, core: 2. Of those that a mesh axis runs over, the one named last changes fastest.
Arguments:
- tokens: bfloat16 [8192, 8192], P(('grp', 'fsdp')), may hold values from -6 to 6
- cotangent: bfloat16 [8192, 16384], P(('grp', 'fsdp')), may hold values from -6 to 6
- adapter_a: float32 [16, 16, 8192], P(None, None, 'fsdp'), may hold values from -0.0625 to 0.0625
- adapter_b: float32 [16, 16, 16384], P(None, None, 'fsdp'), may hold values from -1.5 to 1.5
- block_map: int32 [64], replicated, may hold values from 0 to 15, as said below
- adapter_owner: int32 [16], replicated, may hold values from 0 to 3, as said below
Outputs:
- delta: bfloat16 [8192, 16384], P(('grp', 'fsdp'))
- grad_tokens: bfloat16 [8192, 8192], P(('grp', 'fsdp'))
- grad_down: float32 [32, 16, 8192], P('grp', None, 'fsdp')
- grad_up: float32 [32, 16, 16384], P('grp', None, 'fsdp')
Inputs may be any that keep to these rules, and one draw needn't show every extreme that they name: `block_map`: the 16 blocks of each group (blocks g * 16 to (g + 1) * 16 - 1) name exactly 4 distinct adapters. `adapter_owner`: no group owns more than 8 adapters, and one group owns exactly 8.
All inputs are finite; a program needn't handle non-finite values.
Results may differ from a plain program's by a relative error of at most 0.0065.
Values may be sent and summed in bfloat16 or wider, within the bound.
A program may use at most 128 MiB of HBM per device.

v0:
```python
import functools

import jax
import jax.numpy as jnp
from jax import lax
from jax.experimental import pallas as pl
from jax.experimental.pallas import tpu as pltpu
from jax.sharding import PartitionSpec as P

BLOCK = 128
USED = 4
OWN_MAX = 8
RANK = 16
ROWS = USED * RANK
MESH = pl.DeviceIdType.MESH
NT = (((1,), (1,)), ((), ()))
PIECES = 3
RIGHT, LEFT, PARTNER = 0, 1, 2


def used_adapters(bm, base, count, last_name):
    found = []
    for _ in range(USED):
        def smallest(i, best, last=found[-1] if found else -1):
            entry = bm[base + i]
            return jnp.where((entry > last) & (entry < best), entry, best)

        found.append(lax.fori_loop(0, count, smallest, jnp.int32(last_name), unroll=min(count, 16)))
    return found


def exchange(
    groups, shards,
    bm, owners, a_hbm, b_hbm,
    mask_out, pick_out, scale_out, wd_out, wu_out,
    a_f32, b_f32, wd, wu, load_sem, store_sem, ag_send, ag_recv,
):
    line = shards // 2
    g = lax.axis_index("grp")
    f = lax.axis_index("fsdp")
    z = f // 2
    c = f % 2
    mate = z * 2 + (1 - c)
    wp = a_hbm.shape[2]
    rows = mask_out.shape[0]
    blocks_dev = rows // BLOCK
    total_blocks = bm.shape[0]
    group_blocks = total_blocks // groups
    adapters = a_hbm.shape[0]

    barrier = pltpu.get_barrier_semaphore()
    pl.semaphore_signal(barrier, inc=1, device_id=(g, mate), device_id_type=MESH)
    for step in range(1, line):
        pl.semaphore_signal(
            barrier, inc=1, device_id=(g, ((z + step) % line) * 2 + c), device_id_type=MESH
        )
    for step in range(1, groups):
        pl.semaphore_signal(
            barrier, inc=1, device_id=((g + step) % groups, f), device_id_type=MESH
        )
    load_a = pltpu.make_async_copy(a_hbm, a_f32, load_sem.at[0])
    load_b = pltpu.make_async_copy(b_hbm, b_f32, load_sem.at[1])
    load_a.start()
    load_b.start()

    used = used_adapters(bm, g * group_blocks, group_blocks, adapters - 1)

    def weights(piece, shard):
        return wd.at[shard] if piece == 0 else wu.at[piece - 1, shard]

    endings = []

    def send(cond, build):
        if cond is None:
            build().start()
            endings.append(lambda: build().wait_send())
            return

        @pl.when(cond)
        def _():
            build().start()

        def finish():
            @pl.when(cond)
            def _():
                build().wait_send()

        endings.append(finish)

    def gather_copy(piece, origin, way):
        ref = weights(piece, origin)
        target = {RIGHT: f + 2, LEFT: f - 2, PARTNER: mate}[way]
        return pltpu.make_async_remote_copy(
            src_ref=ref, dst_ref=ref,
            send_sem=ag_send.at[way, piece, origin // 2],
            recv_sem=ag_recv.at[piece, origin],
            device_id=(g, target), device_id_type=MESH,
        )

    def gather_send(piece, origin, way, cond):
        send(cond, lambda: gather_copy(piece, origin, way))

    def gather_own(piece):
        gather_send(piece, f, RIGHT, z < line - 1)
        gather_send(piece, f, LEFT, z > 0)
        gather_send(piece, f, PARTNER, None)

    def gather_step(piece, dist):
        for sign in (-1, 1):
            here = (z - dist >= 0) if sign < 0 else (z + dist < line)
            origin = (z + sign * dist) * 2 + c
            onward = (z < line - 1) if sign < 0 else (z > 0)

            @pl.when(here)
            def _():
                gather_copy(piece, origin, PARTNER).wait_recv()

            gather_send(piece, origin, RIGHT if sign < 0 else LEFT, here & onward)
            gather_send(piece, origin, PARTNER, here)
    def gather_mates(piece, dists):
        for dist in dists:
            for sign in (-1, 1) if dist else (1,):
                here = (z - dist >= 0) if sign < 0 else (z + dist < line)
                origin = (z + sign * dist) * 2 + (1 - c)

                @pl.when(here)
                def _():
                    gather_copy(piece, origin, PARTNER).wait_recv()

    def masked(acc):
        row = lax.broadcasted_iota(jnp.int32, (rows, ROWS), 0) // BLOCK
        slot = lax.broadcasted_iota(jnp.int32, (rows, ROWS), 1) // RANK
        wanted = jnp.zeros((rows, ROWS), jnp.int32)
        for b in range(blocks_dev):
            entry = bm[(g * shards + f) * blocks_dev + b]
            place = jnp.int32(0)
            for s in range(1, USED):
                place = jnp.where(entry == used[s], s, place)
            wanted = jnp.where(row == b, place, wanted)
        return jnp.where(slot == wanted, acc, 0.0)

    load_a.wait()
    wd[f] = jnp.concatenate([a_f32[u].astype(jnp.bfloat16) for u in used], axis=0)
    pl.semaphore_wait(barrier, line + groups - 1)
    gather_own(0)
    load_b.wait()
    for half in range(2):
        wu[half, f] = jnp.concatenate(
            [b_f32[u, :, half * wp:(half + 1) * wp].astype(jnp.bfloat16) for u in used], axis=0
        )
    for dist in range(1, line):
        gather_step(0, dist)
        if dist == 1:
            gather_own(1)
    for dist in range(1, line):
        gather_step(1, dist)
        if dist == 1:
            gather_own(2)
    for dist in range(1, line):
        gather_step(2, dist)
    for piece in range(PIECES):
        gather_mates(piece, range(line))
    mask_out[...] = masked(jnp.ones((rows, ROWS), jnp.float32))
    store_d = pltpu.make_async_copy(wd, wd_out, store_sem.at[0])
    store_u = pltpu.make_async_copy(wu, wu_out, store_sem.at[1])
    store_d.start()
    store_u.start()

    names = [
        used_adapters(bm, other * group_blocks, group_blocks, adapters - 1)
        for other in range(groups)
    ]
    owned = [jnp.int32(-1)] * OWN_MAX
    position = jnp.int32(0)
    for a in range(adapters):
        mine = owners[a] == g
        for k in range(OWN_MAX):
            owned[k] = jnp.where(mine & (position == k), a, owned[k])
        position = position + jnp.where(mine, 1, 0)

    def count(i, totals):
        entry = bm[i]
        return tuple(n + jnp.where(entry == o, 1, 0) for n, o in zip(totals, owned))

    totals = lax.fori_loop(0, total_blocks, count, (jnp.int32(0),) * OWN_MAX, unroll=8)
    shape = (OWN_MAX * RANK, groups * ROWS)
    row = lax.broadcasted_iota(jnp.int32, shape, 0)
    col = lax.broadcasted_iota(jnp.int32, shape, 1)
    row_name = jnp.full(shape, -1, jnp.int32)
    col_name = jnp.full(shape, -2, jnp.int32)
    for k in range(OWN_MAX):
        row_name = jnp.where(row // RANK == k, owned[k], row_name)
    for q in range(groups * USED):
        col_name = jnp.where(col // RANK == q, names[q // USED][q % USED], col_name)
    hit = (row % RANK == col % RANK) & (row_name == col_name)
    pick_out[...] = jnp.where(hit, 1.0, 0.0).astype(jnp.bfloat16)
    wide = lax.broadcasted_iota(jnp.int32, scale_out.shape, 0) // RANK
    uses = jnp.zeros(scale_out.shape, jnp.int32)
    for k in range(OWN_MAX):
        uses = jnp.where(wide == k, totals[k], uses)
    scale_out[...] = 1.0 / (BLOCK * jnp.maximum(uses, 1)).astype(jnp.float32)
    store_d.wait()
    store_u.wait()
    for finish in endings:
        finish()


def outputs(low, back, pick, scale, wd, wu, gd, gu, delta, grad_tokens, grad_down, grad_up):
    wp = wd.shape[2]
    for half in range(2):
        delta[:, half * wp:(half + 1) * wp] = jnp.dot(
            low[...], wu[half, 0], preferred_element_type=jnp.float32
        ).astype(delta.dtype)
    grad_tokens[...] = jnp.dot(back[...], wd[0], preferred_element_type=jnp.float32).astype(
        grad_tokens.dtype
    )

    @pl.when(pl.program_id(0) == 0)
    def _():
        for k in range(OWN_MAX):
            span = pl.ds(k * RANK, RANK)
            chosen, factor = pick[span, :], scale[span, 0:1]
            total = jnp.dot(chosen, gd[...], preferred_element_type=jnp.float32)
            grad_down[k] = total * factor
            for half in range(2):
                total = jnp.dot(chosen, gu[half], preferred_element_type=jnp.float32)
                grad_up[k, :, half * wp:(half + 1) * wp] = total * factor


def on_device(groups, shards, tokens, cotangent, adapter_a, adapter_b, block_map, adapter_owner):
    rows, width = tokens.shape
    hidden = cotangent.shape[1]
    wp = adapter_a.shape[2]
    assert adapter_b.shape[2] == 2 * wp
    line = shards // 2
    bf16, f32 = jnp.bfloat16, jnp.float32
    dma = pltpu.SemaphoreType.DMA
    vmem = pl.BlockSpec(memory_space=pltpu.VMEM)
    smem = pl.BlockSpec(memory_space=pltpu.SMEM)
    anywhere = pl.BlockSpec(memory_space=pl.ANY)
    mask, pick, scale, wd, wu = pl.pallas_call(
        functools.partial(exchange, groups, shards),
        name="exchange",
        out_shape=(
            jax.ShapeDtypeStruct((rows, ROWS), f32),
            jax.ShapeDtypeStruct((OWN_MAX * RANK, groups * ROWS), bf16),
            jax.ShapeDtypeStruct((OWN_MAX * RANK, 128), f32),
            jax.ShapeDtypeStruct((shards, ROWS, wp), bf16),
            jax.ShapeDtypeStruct((2, shards, ROWS, wp), bf16),
        ),
        in_specs=[smem, smem] + [anywhere] * 2,
        out_specs=(vmem, vmem, vmem, anywhere, anywhere),
        scratch_shapes=[
            pltpu.VMEM(adapter_a.shape, f32),
            pltpu.VMEM(adapter_b.shape, f32),
            pltpu.VMEM((shards, ROWS, wp), bf16),
            pltpu.VMEM((2, shards, ROWS, wp), bf16),
            dma((2,)),
            dma((2,)),
            dma((3, PIECES, line)),
            dma((PIECES, shards)),
        ],
        compiler_params=pltpu.CompilerParams(
            collective_id=0, has_side_effects=True, vmem_limit_bytes=58 * 1024 * 1024
        ),
    )(block_map, adapter_owner, adapter_a, adapter_b)
    down = wd.transpose(1, 0, 2).reshape(ROWS, width)
    up = wu.transpose(2, 1, 0, 3).reshape(ROWS, hidden)
    on = mask > 0.5

    def ranks(values, maps):
        total = lax.dot_general(values, maps, NT, preferred_element_type=f32)
        return jnp.where(on, total, 0.0).astype(bf16)

    def summed(left, values, size):
        part = lax.dot_general(
            left, values, (((0,), (0,)), ((), ())), preferred_element_type=f32
        ).astype(bf16)
        part = part.reshape(ROWS, shards, size).transpose(1, 0, 2)
        share = lax.psum_scatter(part, "fsdp", scatter_dimension=0, tiled=True)
        return lax.all_gather(share[0], "grp", axis=0)

    low = ranks(tokens, down)
    back = ranks(cotangent, up)
    gd = summed(back, tokens, wp)
    gu = summed(low, cotangent, 2 * wp).reshape(groups, ROWS, 2, wp).transpose(2, 0, 1, 3)
    gd = gd.reshape(groups * ROWS, wp)
    gu = gu.reshape(2, groups * ROWS, wp)
    whole = lambda shape: pl.BlockSpec(shape, lambda i: (0,) * len(shape))
    delta, grad_tokens, grad_down, grad_up = pl.pallas_call(
        outputs,
        name="outputs",
        grid=(shards,),
        out_shape=(
            jax.ShapeDtypeStruct((rows, hidden), bf16),
            jax.ShapeDtypeStruct((rows, width), bf16),
            jax.ShapeDtypeStruct((OWN_MAX, RANK, wp), f32),
            jax.ShapeDtypeStruct((OWN_MAX, RANK, 2 * wp), f32),
        ),
        in_specs=[
            whole(low.shape), whole(back.shape), whole(pick.shape), whole(scale.shape),
            pl.BlockSpec((1, ROWS, wp), lambda i: (i, 0, 0)),
            pl.BlockSpec((2, 1, ROWS, wp), lambda i: (0, i, 0, 0)),
            whole(gd.shape), whole(gu.shape),
        ],
        out_specs=(
            pl.BlockSpec((rows, 2 * wp), lambda i: (0, i)),
            pl.BlockSpec((rows, wp), lambda i: (0, i)),
            whole((OWN_MAX, RANK, wp)), whole((OWN_MAX, RANK, 2 * wp)),
        ),
    )(low, back, pick, scale, wd, wu, gd, gu)
    return delta, grad_tokens, grad_down, grad_up


def solution(mesh):
    placed = (
        P(("grp", "fsdp"), None),
        P(("grp", "fsdp"), None),
        P(None, None, "fsdp"),
        P(None, None, "fsdp"),
        P(),
        P(),
    )
    return jax.shard_map(
        functools.partial(on_device, mesh.shape["grp"], mesh.shape["fsdp"]),
        mesh=mesh,
        in_specs=placed,
        out_specs=(
            P(("grp", "fsdp"), None),
            P(("grp", "fsdp"), None),
            P("grp", None, "fsdp"),
            P("grp", None, "fsdp"),
        ),
        check_vma=False,
    )
```

profile of v0, /device:TPU:0, one launch (start us, length us, event | category | flops | bytes accessed | tf_op | source)
XLA Modules:
  0.0 172.8 jit_solution(640542188608431979)
XLA Ops:
  7.2 0.0 reduce-scatter.5.cloned.1.call-start
  7.2 0.0 copy-start
  7.2 36.9 %exchange.1 = (f32[256,64]{1,0:T(8,128)}, bf16[128,256]{1,0:T(8,128)(2,1)}, f32[128,128]{1,0:T(8,128)}, bf16[8,64,1024]{2,1,0:T(8,128)(2,1)}, bf16[2,8,64,1024]{3,2,1,0:T(8,128)(2,1)}) custom-call(s32[64]{0:T(128)} %bm.1, s32[16]{0:T(128)} %owners.1, f32[16,16,1024]{2,1,0:T(8,128)} %a_hbm.1, f32[16,16,2048]{2,1,0:T(8,128)} %b_hbm.1), custom_call_target="tpu_custom_call" | custom-call | tf_op jit(solution)/shard_map/exchange/pallas_call | solution.py:241
  44.2 0.9 broadcast_compare_fusion
  45.1 1.3 copy.31
  46.4 0.0 copy-done
  46.4 1.3 fusion.3.low
  47.7 0.0 copy-start.3
  47.7 5.0 %convolution_convert_fusion = bf16[64,16384]{1,0:T(8,128)(2,1)S(1)} fusion(bf16[256,64]{1,0:T(8,128)(2,1)S(1)} %fusion.3.low, bf16[256,16384]{1,0:T(8,128)(2,1)} %param.7), kind=kOutput, calls=%fused_computation | convolution fusion | flops 537919488 | bytes 10518528 | tf_op jit(solution)/shard_map/dot_general | solution.py:276
  52.7 0.0 copy-done.3
  52.7 0.0 copy-start.2
  52.8 1.5 copy.34
  54.2 0.0 reduce-scatter.5.cloned.1.call-update
  54.2 0.0 reduce-scatter.3.cloned.1.call-start
  54.3 0.8 copy-done.2
  55.1 3.5 %copy.22 = bf16[64,8,2,1024]{3,2,1,0:T(2,128)(2,1)} copy(bf16[64,8,2,1024]{3,0,1,2:T(8,128)(2,1)S(1)} %bitcast.42) | data formatting | bytes 4194304 | tf_op jit(solution)/shard_map/transpose | solution.py:268
  58.6 3.3 %reshape.30 = bf16[64,16384]{1,0:T(8,128)(2,1)S(1)} reshape(bf16[64,8,2,1024]{3,2,1,0:T(2,128)(2,1)} %copy.22) | data formatting | bytes 4194304 | tf_op jit(solution)/shard_map/reshape | solution.py:268
  61.9 0.0 copy-start.1
  61.9 5.8 %fusion.2.back = bf16[256,64]{1,0:T(8,128)(2,1)S(1)} fusion(pred[256,64]{1,0:T(32,128)(4,1)S(1)} %broadcast_compare_fusion, bf16[64,16384]{1,0:T(8,128)(2,1)S(1)} %reshape.30, bf16[256,16384]{1,0:T(8,128)(2,1)} %param.7), kind=kOutput, calls=%fused_computation.7 | convolution fusion | flops 536903680 | bytes 10534912 | tf_op jit(solution)/shard_map/dot_general | solution.py:272
  67.8 0.0 copy-done.1
  67.8 0.0 copy-start.4
  67.8 0.9 convolution_convert_fusion.1
  68.7 1.1 copy.35
  69.7 0.0 reduce-scatter.3.cloned.1.call-update
  69.7 0.0 copy-done.4
  69.7 0.0 all-gather.2.cloned.1.call-start
  69.8 20.1 %reduce-scatter.5.cloned.1.call-done = bf16[1,64,2048]{2,1,0:T(8,128)(2,1)} async-done(((bf16[8,64,2048]{2,1,0:T(8,128)(2,1)}), bf16[1,64,2048]{2,1,0:T(8,128)(2,1)}) %reduce-scatter.5.cloned.1.call-update) | async-done | bytes 262160 | tf_op jit(solution)/shard_map/reduce_scatter | solution.py:280
  89.9 0.0 all-gather.2.cloned.1.call-update
  90.0 34.3 %reduce-scatter.3.cloned.1.call-done = bf16[1,64,1024]{2,1,0:T(8,128)(2,1)} async-done(((bf16[8,64,1024]{2,1,0:T(8,128)(2,1)}), bf16[1,64,1024]{2,1,0:T(8,128)(2,1)}) %reduce-scatter.3.cloned.1.call-update) | async-done | bytes 131088 | tf_op jit(solution)/shard_map/reduce_scatter | solution.py:280
  124.2 14.3 %all_gather.6 = bf16[4,64,1024]{2,1,0:T(8,128)(2,1)} all-gather(bf16[1,64,1024]{2,1,0:T(8,128)(2,1)} %reduce-scatter.3.cloned.1.call-done), channel_id=1, replica_groups=mesh['grp'=4,'fsdp'=8] {'grp'}, dimensions={0}, use_global_device_ids=true | all-gather | bytes 655360 | tf_op jit(solution)/shard_map/all_gather | solution.py:281
  138.6 12.2 %all-gather.2.cloned.1.call-done = bf16[4,64,2048]{2,1,0:T(8,128)(2,1)} async-done(((bf16[1,64,2048]{2,1,0:T(8,128)(2,1)}), bf16[4,64,2048]{2,1,0:T(8,128)(2,1)}) %all-gather.2.cloned.1.call-update) | async-done | bytes 1048592 | tf_op jit(solution)/shard_map/all_gather | solution.py:281
  150.7 1.8 %reshape.34 = bf16[4,64,2,1024]{3,2,1,0:T(2,128)(2,1)S(1)} reshape(bf16[4,64,2048]{2,1,0:T(8,128)(2,1)} %all-gather.2.cloned.1.call-done) | data formatting | bytes 2097152 | tf_op jit(solution)/shard_map/reshape | solution.py:286
  152.6 1.3 copy.26
  153.9 12.4 %outputs.1 = (bf16[256,16384]{1,0:T(8,128)(2,1)}, bf16[256,8192]{1,0:T(8,128)(2,1)}, f32[8,16,1024]{2,1,0:T(8,128)}, f32[8,16,2048]{2,1,0:T(8,128)}) custom-call(bf16[256,64]{1,0:T(8,128)(2,1)} %copy-done.3, bf16[256,64]{1,0:T(8,128)(2,1)} %copy-done.4, bf16[128,256]{1,0:T(8,128)(2,1)} %get-tuple-element.12.pick, f32[128,128]{1,0:T(8,128)} %get-tuple-element.13.scale, ...), custom_call_target="tpu_custom_call" | custom-call | tf_op jit(solution)/shard_map/outputs/pallas_call | solution.py:290
Async XLA Ops:
  7.2 82.8 %reduce-scatter.5.cloned.1.call-start = ((), (), s32[]{:S(2)}) async-start(), calls=%async_computation.3 | async-start | bytes 2359296 | tf_op jit(solution)/shard_map/reduce_scatter | solution.py:280
  7.2 39.2 %copy-start = (bf16[256,8192]{1,0:T(8,128)(2,1)S(1)}, bf16[256,8192]{1,0:T(8,128)(2,1)}, u32[]{:S(2)}) copy-start(bf16[256,8192]{1,0:T(8,128)(2,1)} %param.6) | copy-start | bytes 12582916
  47.7 5.0 %copy-start.3 = (bf16[256,64]{1,0:T(8,128)(2,1)}, bf16[256,64]{1,0:T(8,128)(2,1)S(1)}, u32[]{:S(2)}) copy-start(bf16[256,64]{1,0:T(8,128)(2,1)S(1)} %fusion.3.low) | copy-start | bytes 98308
  52.7 2.3 %copy-start.2 = (bf16[2,8,64,1024]{3,2,1,0:T(8,128)(2,1)S(1)}, bf16[2,8,64,1024]{3,2,1,0:T(8,128)(2,1)}, u32[]{:S(2)}) copy-start(bf16[2,8,64,1024]{3,2,1,0:T(8,128)(2,1)} %get-tuple-element.11.wu) | copy-start | bytes 6291460
  54.2 70.0 %reduce-scatter.3.cloned.1.call-start = ((), (), s32[]{:S(2)}) async-start(), calls=%async_computation.2 | async-start | bytes 1179648 | tf_op jit(solution)/shard_map/reduce_scatter | solution.py:280
  61.9 5.9 %copy-start.1 = (bf16[256,8192]{1,0:T(8,128)(2,1)S(1)}, bf16[256,8192]{1,0:T(8,128)(2,1)}, u32[]{:S(2)}) copy-start(bf16[256,8192]{1,0:T(8,128)(2,1)} %param.6) | copy-start | bytes 12582916
  67.8 2.0 %copy-start.4 = (bf16[256,64]{1,0:T(8,128)(2,1)}, bf16[256,64]{1,0:T(8,128)(2,1)S(1)}, u32[]{:S(2)}) copy-start(bf16[256,64]{1,0:T(8,128)(2,1)S(1)} %fusion.2.back) | copy-start | bytes 98308
  69.7 81.0 %all-gather.2.cloned.1.call-start = ((), (), s32[]{:S(2)}) async-start(), calls=%async_computation.4 | async-start | bytes 1310720 | tf_op jit(solution)/shard_map/all_gather | solution.py:281
Sparse Core Ops, SparseCore 0:
  54.4 35.5 reduce-scatter.4
  92.8 31.4 reduce-scatter.2
  126.1 24.6 all-gather.1
where the time goes:
time: 173 us
  waiting for transfers between devices  66.6 us (38%)
  Pallas kernels  49.4 us (29%)
  local copies, waits for them, and re-layouts  14.6 us (8%)
  blocking collectives  14.3 us (8%)
  between operations  13.9 us (8%)
  matrix products  13 us (8%)
    reduce_scatter x2, waiting for transfers between devices, summed(): share = lax.psum_scatter(part, 'fsdp', scatter_dimension=0, tiled=True)  54.4 us
    pallas_call x1, Pallas kernels, on_device(): pl.pallas_call(functools.partial(exchange, groups, shards), name='exchang...  36.9 us
    all_gather x1, blocking collectives, summed(): return lax.all_gather(share[0], 'grp', axis=0)  14.3 us
    pallas_call x1, Pallas kernels, on_device(): pl.pallas_call(outputs, name='outputs', grid=(shards,), out_shape=(jax.Sh...  12.4 us
    all_gather x1, waiting for transfers between devices, summed(): return lax.all_gather(share[0], 'grp', axis=0)  12.2 us
    dot_general x2, matrix products, ranks(): total = lax.dot_general(values, maps, NT, preferred_element_type=f32)  7.1 us
    dot_general x2, matrix products, summed(): lax.dot_general(left, values, (((0,), (0,)), ((), ())), preferred_element...  5.89 us
    transpose x1, local copies, waits for them, and re-layouts, on_device(): up = wu.transpose(2, 1, 0, 3).reshape(ROWS, hidden)  3.49 us
  transfers between devices with their start and end apart: 3, of which 3 were waited for; matrix products, arithmetic and copies ran while one was open for 8% of the time, Pallas kernels for 0%

commit v1 on v0

v1 whole, which is shorter than its diff:
```python
import functools

import jax
import jax.numpy as jnp
from jax import lax
from jax.experimental import pallas as pl
from jax.experimental.pallas import tpu as pltpu
from jax.sharding import PartitionSpec as P

BLOCK = 128
USED = 4
OWN_MAX = 8
RANK = 16
ROWS = USED * RANK
MESH = pl.DeviceIdType.MESH
NT = (((1,), (1,)), ((), ()))
PIECES = 3
RIGHT, LEFT, PARTNER = 0, 1, 2
BF16, F32 = jnp.bfloat16, jnp.float32


def used_adapters(bm, base, count, last_name):
    found = []
    for _ in range(USED):
        def smallest(i, best, last=found[-1] if found else -1):
            entry = bm[base + i]
            return jnp.where((entry > last) & (entry < best), entry, best)

        found.append(lax.fori_loop(0, count, smallest, jnp.int32(last_name), unroll=min(count, 16)))
    return found


def exchange(
    groups, shards,
    bm, owners, a_hbm, b_hbm, tokens, cotangent,
    low_out, back_out, pick_out, scale_out, wd_out, wu_out, shares_out,
    a_f32, b_f32, wd, wu_low, wu_high, tok, cot, acc, left_t,
    to_mate, from_mate, own_part, arrived, running, final,
    load_sem, tok_sem, cot_sem, store_sem, ag_send, ag_recv,
    mate_send, mate_recv, run_send, run_recv, grp_send, grp_recv, keep_sem,
):
    line = shards // 2
    g = lax.axis_index("grp")
    f = lax.axis_index("fsdp")
    z = f // 2
    c = f % 2
    mate = z * 2 + (1 - c)
    wp = a_hbm.shape[2]
    rows = tokens.shape[0]
    blocks_dev = rows // BLOCK
    total_blocks = bm.shape[0]
    group_blocks = total_blocks // groups
    adapters = a_hbm.shape[0]
    has_left, has_right = z > 0, z < line - 1
    at_end = (z == 0) | (z == line - 1)

    maps = (wd, wu_low, wu_high)

    barrier = pltpu.get_barrier_semaphore()

    def greet(target):
        pl.semaphore_signal(barrier, inc=1, device_id=target, device_id_type=MESH)

    greet((g, mate))
    pl.when(has_left)(lambda: greet((g, f - 2)))
    pl.when(has_right)(lambda: greet((g, f + 2)))
    for step in range(1, groups):
        greet(((g + step) % groups, f))

    load_a = pltpu.make_async_copy(a_hbm, a_f32, load_sem.at[0])
    load_b = pltpu.make_async_copy(b_hbm, b_f32, load_sem.at[1])
    load_a.start()
    load_b.start()

    def load_tok(s):
        return pltpu.make_async_copy(
            tokens.at[:, pl.ds(pl.multiple_of(s * wp, 128), wp)], tok.at[s], tok_sem.at[s]
        )

    def load_cot(s):
        return pltpu.make_async_copy(
            cotangent.at[:, pl.ds(pl.multiple_of(s * 2 * wp, 128), 2 * wp)], cot.at[s], cot_sem.at[s]
        )

    for s in range(shards):
        load_tok(s).start()
    for s in range(shards):
        load_cot(s).start()

    used = used_adapters(bm, g * group_blocks, group_blocks, adapters - 1)

    def weights(piece, shard):
        return maps[piece].at[shard]

    def gather_copy(piece, origin, way):
        ref = weights(piece, origin)
        target = {RIGHT: f + 2, LEFT: f - 2, PARTNER: mate}[way]
        return pltpu.make_async_remote_copy(
            src_ref=ref, dst_ref=ref,
            send_sem=ag_send.at[way, piece, origin // 2],
            recv_sem=ag_recv.at[piece, origin],
            device_id=(g, target), device_id_type=MESH,
        )

    def gather_own(piece):
        pl.when(has_right)(lambda: gather_copy(piece, f, RIGHT).start())
        pl.when(has_left)(lambda: gather_copy(piece, f, LEFT).start())
        gather_copy(piece, f, PARTNER).start()

    def accumulate(piece):
        def body(s, _):
            if piece == 0:
                values = tok[s]
            else:
                values = cot[s, :, (piece - 1) * wp:piece * wp]
            acc[...] += lax.dot_general(values, maps[piece][s], NT, preferred_element_type=F32)
            return 0

        lax.fori_loop(0, shards, body, 0, unroll=4)

    def gather_span(piece, first, last):
        def body(q, _):
            same = 1 - (q % 4) // 2
            side = 2 * (q % 2) - 1
            dist = q // 4 + same
            place = z + side * dist
            here = (place >= 0) & (place < line) & ((side < 0) | (dist > 0))
            origin = place * 2 + (c + 1 - same) % 2

            @pl.when(here)
            def _():
                gather_copy(piece, origin, PARTNER).wait_recv()

                @pl.when((same == 1) & (side < 0) & has_right)
                def _():
                    gather_copy(piece, origin, RIGHT).start()

                @pl.when((same == 1) & (side > 0) & has_left)
                def _():
                    gather_copy(piece, origin, LEFT).start()

                @pl.when(same == 1)
                def _():
                    gather_copy(piece, origin, PARTNER).start()

            return 0

        lax.fori_loop(first, last, body, 0)

    def gather_finish(piece):
        def body(place, _):
            origin = place * 2 + c
            pl.when((place <= z) & has_right)(
                lambda: gather_copy(piece, origin, RIGHT).wait_send()
            )
            pl.when((place >= z) & has_left)(
                lambda: gather_copy(piece, origin, LEFT).wait_send()
            )
            gather_copy(piece, origin, PARTNER).wait_send()
            return 0

        lax.fori_loop(0, line, body, 0)

    def masked(total):
        row = lax.broadcasted_iota(jnp.int32, (rows, ROWS), 0) // BLOCK
        slot = lax.broadcasted_iota(jnp.int32, (rows, ROWS), 1) // RANK
        wanted = jnp.zeros((rows, ROWS), jnp.int32)
        for b in range(blocks_dev):
            entry = bm[(g * shards + f) * blocks_dev + b]
            place = jnp.int32(0)
            for s in range(1, USED):
                place = jnp.where(entry == used[s], s, place)
            wanted = jnp.where(row == b, place, wanted)
        return jnp.where(slot == wanted, total, 0.0)

    steps = [(side, dist) for dist in range(line - 1, 0, -1) for side in (1, -1)] + [(1, 0)]
    number = {step: i for i, step in enumerate(steps)}
    last = number[(1, 0)]

    def here(step):
        side, dist = step
        return z + dist < line if side > 0 else z - dist >= 0

    def mate_copy(p, i):
        return pltpu.make_async_remote_copy(
            src_ref=to_mate.at[p, i], dst_ref=from_mate.at[p, i],
            send_sem=mate_send.at[p, i], recv_sem=mate_recv.at[p, i],
            device_id=(g, mate), device_id_type=MESH,
        )

    def partials(pieces, values):
        for i, (side, dist) in enumerate(steps):
            d = z + side * dist

            @pl.when(here((side, dist)))
            def _():
                given = jnp.dot(
                    left_t[...], values[d * 2 + (1 - c)], preferred_element_type=F32
                )
                for n, p in enumerate(pieces):
                    to_mate[p, i] = given[:, n * wp:(n + 1) * wp].astype(BF16)
                for p in pieces:
                    mate_copy(p, i).start()
                kept = jnp.dot(left_t[...], values[d * 2 + c], preferred_element_type=F32)
                for n, p in enumerate(pieces):
                    own_part[p, i] = kept[:, n * wp:(n + 1) * wp]

    def run_copy(p, side, dist):
        row = (1 - side) // 2
        return pltpu.make_async_remote_copy(
            src_ref=running.at[p, number[(side, dist)]], dst_ref=arrived.at[p, row, dist - 1],
            send_sem=run_send.at[p, number[(side, dist)]], recv_sem=run_recv.at[p, row, dist - 1],
            device_id=(g, f + 2 * side), device_id_type=MESH,
        )

    def run_wait(p, side, dist):
        run_copy(p, side, dist + 1).wait_recv()
        return arrived[p, (1 - side) // 2, dist].astype(F32)

    def pass_on(pieces):
        for i, (side, dist) in enumerate(steps[:-1]):
            fed = has_left if side > 0 else has_right

            @pl.when(here((side, dist)))
            def _():
                for p in pieces:
                    mate_copy(p, i).wait_recv()
                    if dist < line - 1:
                        @pl.when(fed)
                        def _():
                            running[p, i] = (
                                own_part[p, i]
                                + from_mate[p, i].astype(F32)
                                + run_wait(p, side, dist)
                            ).astype(BF16)

                        @pl.when(jnp.logical_not(fed))
                        def _():
                            running[p, i] = (
                                own_part[p, i] + from_mate[p, i].astype(F32)
                            ).astype(BF16)
                    else:
                        running[p, i] = (own_part[p, i] + from_mate[p, i].astype(F32)).astype(
                            BF16
                        )
                    run_copy(p, side, dist).start()

    def grp_copy(p, step):
        return pltpu.make_async_remote_copy(
            src_ref=final.at[p], dst_ref=shares_out.at[p, g],
            send_sem=grp_send.at[p, step], recv_sem=grp_recv.at[p, g],
            device_id=((g + step) % groups, f), device_id_type=MESH,
        )

    def grp_wait(p, other):
        pltpu.make_async_remote_copy(
            src_ref=final.at[p], dst_ref=shares_out.at[p, other],
            send_sem=grp_send.at[p, 0], recv_sem=grp_recv.at[p, other],
            device_id=(g, mate), device_id_type=MESH,
        ).wait_recv()

    def keep_copy(p):
        return pltpu.make_async_copy(final.at[p], shares_out.at[p, g], keep_sem.at[p])

    def finish_piece(p):
        mate_copy(p, last).wait_recv()
        own_part[p, last] += from_mate[p, last].astype(F32)

        @pl.when(has_left)
        def _():
            own_part[p, last] += run_wait(p, 1, 0)

        @pl.when(has_right)
        def _():
            own_part[p, last] += run_wait(p, -1, 0)

        final[p] = own_part[p, last].astype(BF16)
        for step in range(1, groups):
            grp_copy(p, step).start()
        keep_copy(p).start()

    load_a.wait()
    wd[f] = jnp.concatenate([a_f32[u].astype(BF16) for u in used], axis=0)
    pl.semaphore_wait(
        barrier, groups + jnp.where(has_left, 1, 0) + jnp.where(has_right, 1, 0)
    )
    gather_own(0)
    load_b.wait()
    for half in range(2):
        maps[1 + half][f] = jnp.concatenate(
            [b_f32[u, :, half * wp:(half + 1) * wp].astype(BF16) for u in used], axis=0
        )
    acc[...] = jnp.zeros_like(acc)
    gather_span(0, 0, 2)
    gather_own(1)
    gather_span(0, 2, 4 * line)
    gather_own(2)
    for s in range(shards):
        load_tok(s).wait()
    accumulate(0)
    low = masked(acc[...])
    low_out[...] = low.astype(BF16)
    left_t[...] = low.T.astype(BF16)
    for s in range(shards):
        load_cot(s).wait()
    partials((0, 1), cot)
    pl.when(at_end)(lambda: pass_on((0, 1)))

    acc[...] = jnp.zeros_like(acc)
    gather_span(1, 0, 4 * line)
    accumulate(1)
    gather_span(2, 0, 4 * line)
    accumulate(2)
    back = masked(acc[...])
    back_out[...] = back.astype(BF16)
    left_t[...] = back.T.astype(BF16)
    partials((2,), tok)
    pl.when(at_end)(lambda: pass_on((2,)))
    pl.when(jnp.logical_not(at_end))(lambda: pass_on((0, 1)))

    store_d = pltpu.make_async_copy(wd, wd_out, store_sem.at[0])
    store_l = pltpu.make_async_copy(wu_low, wu_out.at[0], store_sem.at[1])
    store_h = pltpu.make_async_copy(wu_high, wu_out.at[1], store_sem.at[2])
    store_d.start()
    store_l.start()
    store_h.start()

    finish_piece(0)
    finish_piece(1)
    pl.when(jnp.logical_not(at_end))(lambda: pass_on((2,)))

    names = [
        used_adapters(bm, other * group_blocks, group_blocks, adapters - 1)
        for other in range(groups)
    ]
    owned = [jnp.int32(-1)] * OWN_MAX
    position = jnp.int32(0)
    for a in range(adapters):
        mine = owners[a] == g
        for k in range(OWN_MAX):
            owned[k] = jnp.where(mine & (position == k), a, owned[k])
        position = position + jnp.where(mine, 1, 0)

    def count(i, totals):
        entry = bm[i]
        return tuple(n + jnp.where(entry == o, 1, 0) for n, o in zip(totals, owned))

    totals = lax.fori_loop(0, total_blocks, count, (jnp.int32(0),) * OWN_MAX, unroll=8)
    shape = (OWN_MAX * RANK, groups * ROWS)
    row = lax.broadcasted_iota(jnp.int32, shape, 0)
    col = lax.broadcasted_iota(jnp.int32, shape, 1)
    row_name = jnp.full(shape, -1, jnp.int32)
    col_name = jnp.full(shape, -2, jnp.int32)
    for k in range(OWN_MAX):
        row_name = jnp.where(row // RANK == k, owned[k], row_name)
    for q in range(groups * USED):
        col_name = jnp.where(col // RANK == q, names[q // USED][q % USED], col_name)
    hit = (row % RANK == col % RANK) & (row_name == col_name)
    pick_out[...] = jnp.where(hit, 1.0, 0.0).astype(BF16)
    wide = lax.broadcasted_iota(jnp.int32, scale_out.shape, 0) // RANK
    uses = jnp.zeros(scale_out.shape, jnp.int32)
    for k in range(OWN_MAX):
        uses = jnp.where(wide == k, totals[k], uses)
    scale_out[...] = 1.0 / (BLOCK * jnp.maximum(uses, 1)).astype(F32)

    finish_piece(2)
    for piece in range(PIECES):
        gather_finish(piece)

    for i, step in enumerate(steps):
        @pl.when(here(step))
        def _():
            for p in range(PIECES):
                mate_copy(p, i).wait_send()
                if i != last:
                    run_copy(p, *step).wait_send()

    store_d.wait()
    store_l.wait()
    store_h.wait()
    for p in range(PIECES):
        keep_copy(p).wait()
        for step in range(1, groups):
            grp_copy(p, step).wait_send()
        for step in range(1, groups):
            grp_wait(p, (g + step) % groups)


def outputs(
    low, back, pick, scale, wd, wu, up_shares, down_shares,
    delta, grad_tokens, grad_down, grad_up,
):
    count, _, wp = wd.shape
    for s in range(count):
        for half in range(2):
            start = (s * 2 + half) * wp
            delta[:, start:start + wp] = jnp.dot(
                low[...], wu[half, s], preferred_element_type=F32
            ).astype(delta.dtype)
        grad_tokens[:, s * wp:(s + 1) * wp] = jnp.dot(
            back[...], wd[s], preferred_element_type=F32
        ).astype(grad_tokens.dtype)
    for shares, grad in ((down_shares, grad_down), (up_shares, grad_up)):
        total = jnp.dot(pick[...], shares[0], preferred_element_type=F32)
        grad[...] = (total * scale[:, 0:1]).reshape(grad.shape)


def on_device(groups, shards, tokens, cotangent, adapter_a, adapter_b, block_map, adapter_owner):
    rows, width = tokens.shape
    hidden = cotangent.shape[1]
    wp = adapter_a.shape[2]
    assert adapter_b.shape[2] == 2 * wp
    line = shards // 2
    dma = pltpu.SemaphoreType.DMA
    vmem = pl.BlockSpec(memory_space=pltpu.VMEM)
    smem = pl.BlockSpec(memory_space=pltpu.SMEM)
    anywhere = pl.BlockSpec(memory_space=pl.ANY)
    low, back, pick, scale, wd, wu, shares = pl.pallas_call(
        functools.partial(exchange, groups, shards),
        name="exchange",
        out_shape=(
            jax.ShapeDtypeStruct((rows, ROWS), BF16),
            jax.ShapeDtypeStruct((rows, ROWS), BF16),
            jax.ShapeDtypeStruct((OWN_MAX * RANK, groups * ROWS), BF16),
            jax.ShapeDtypeStruct((OWN_MAX * RANK, 128), F32),
            jax.ShapeDtypeStruct((shards, ROWS, wp), BF16),
            jax.ShapeDtypeStruct((2, shards, ROWS, wp), BF16),
            jax.ShapeDtypeStruct((PIECES, groups, ROWS, wp), BF16),
        ),
        in_specs=[smem, smem] + [anywhere] * 4,
        out_specs=(vmem,) * 4 + (anywhere,) * 3,
        scratch_shapes=[
            pltpu.VMEM(adapter_a.shape, F32),
            pltpu.VMEM(adapter_b.shape, F32),
            pltpu.VMEM((shards, ROWS, wp), BF16),
            pltpu.VMEM((shards, ROWS, wp), BF16),
            pltpu.VMEM((shards, ROWS, wp), BF16),
            pltpu.VMEM((shards, rows, wp), BF16),
            pltpu.VMEM((shards, rows, 2 * wp), BF16),
            pltpu.VMEM((rows, ROWS), F32),
            pltpu.VMEM((ROWS, rows), BF16),
            pltpu.VMEM((PIECES, 2 * line - 1, ROWS, wp), BF16),
            pltpu.VMEM((PIECES, 2 * line - 1, ROWS, wp), BF16),
            pltpu.VMEM((PIECES, 2 * line - 1, ROWS, wp), F32),
            pltpu.VMEM((PIECES, 2, line, ROWS, wp), BF16),
            pltpu.VMEM((PIECES, 2 * line - 1, ROWS, wp), BF16),
            pltpu.VMEM((PIECES, ROWS, wp), BF16),
            dma((2,)),
            dma((shards,)),
            dma((shards,)),
            dma((3,)),
            dma((3, PIECES, line)),
            dma((PIECES, shards)),
            dma((PIECES, 2 * line - 1)),
            dma((PIECES, 2 * line - 1)),
            dma((PIECES, 2 * line - 1)),
            dma((PIECES, 2, line)),
            dma((PIECES, groups)),
            dma((PIECES, groups)),
            dma((PIECES,)),
        ],
        compiler_params=pltpu.CompilerParams(
            collective_id=0, has_side_effects=True, vmem_limit_bytes=56 * 1024 * 1024
        ),
    )(block_map, adapter_owner, adapter_a, adapter_b, tokens, cotangent)
    shares = shares.reshape(PIECES, groups * ROWS, wp)
    steps = min(4, wp // 128)
    half = steps // 2
    whole = lambda shape: pl.BlockSpec(shape, lambda i: (0,) * len(shape))
    return pl.pallas_call(
        outputs,
        name="outputs",
        grid=(steps,),
        out_shape=(
            jax.ShapeDtypeStruct((rows, hidden), BF16),
            jax.ShapeDtypeStruct((rows, width), BF16),
            jax.ShapeDtypeStruct((OWN_MAX, RANK, wp), F32),
            jax.ShapeDtypeStruct((OWN_MAX, RANK, 2 * wp), F32),
        ),
        in_specs=[
            whole(low.shape), whole(back.shape), whole(pick.shape), whole(scale.shape),
            pl.BlockSpec((shards // steps, ROWS, wp), lambda i: (i, 0, 0)),
            pl.BlockSpec((2, shards // steps, ROWS, wp), lambda i: (0, i, 0, 0)),
            pl.BlockSpec((1, groups * ROWS, wp // half), lambda i: (i // half, 0, i % half)),
            pl.BlockSpec((1, groups * ROWS, wp // steps), lambda i: (2, 0, i)),
        ],
        out_specs=(
            pl.BlockSpec((rows, hidden // steps), lambda i: (0, i)),
            pl.BlockSpec((rows, width // steps), lambda i: (0, i)),
            pl.BlockSpec((OWN_MAX, RANK, wp // steps), lambda i: (0, 0, i)),
            pl.BlockSpec((OWN_MAX, RANK, 2 * wp // steps), lambda i: (0, 0, i)),
        ),
    )(low, back, pick, scale, wd, wu, shares, shares)


def solution(mesh):
    placed = (
        P(("grp", "fsdp"), None),
        P(("grp", "fsdp"), None),
        P(None, None, "fsdp"),
        P(None, None, "fsdp"),
        P(),
        P(),
    )
    return jax.shard_map(
        functools.partial(on_device, mesh.shape["grp"], mesh.shape["fsdp"]),
        mesh=mesh,
        in_specs=placed,
        out_specs=(
            P(("grp", "fsdp"), None),
            P(("grp", "fsdp"), None),
            P("grp", None, "fsdp"),
            P("grp", None, "fsdp"),
        ),
        check_vma=False,
    )
```

time: 173 us -> 81.4 us (0.47)
  waiting for transfers between devices: 66.6 us -> 0 us
  Pallas kernels: 49.4 us -> 80.4 us
  local copies, waits for them, and re-layouts: 14.6 us -> 0 us
  blocking collectives: 14.3 us -> 0 us
  between operations: 13.9 us -> 0.64 us
  matrix products: 13 us -> 0 us
    reduce_scatter x2 -> x0, waiting for transfers between devices: 54.4 us -> none  [summed(): share = lax.psum_scatter(part, 'fsdp', scatter_dimension=0, tiled=True)]
    pallas_call x1, Pallas kernels: 36.9 us -> 71.7 us  [on_device(): pl.pallas_call(functools.partial(exchange, groups, shards), name='exchang...]
    all_gather x1 -> x0, blocking collectives: 14.3 us -> none  [summed(): return lax.all_gather(share[0], 'grp', axis=0)]
    dot_general x4 -> x0, matrix products: 13 us -> none  [the longest x2 7.1 us: ranks(): total = lax.dot_general(values, maps, NT, preferred_element_type=f32)]
    all_gather x1 -> x0, waiting for transfers between devices: 12.2 us -> none  [summed(): return lax.all_gather(share[0], 'grp', axis=0)]
    reshape x5 -> x0, local copies, waits for them, and re-layouts: 8.95 us -> none  [the longest x1 3.3 us: on_device(): up = wu.transpose(2, 1, 0, 3).reshape(ROWS, hidden)]
    transpose x2 -> x0, local copies, waits for them, and re-layouts: 4.76 us -> none  [the longest x1 3.49 us: on_device(): up = wu.transpose(2, 1, 0, 3).reshape(ROWS, hidden)]
    pallas_call x1, Pallas kernels: 12.4 us -> 8.68 us  [on_device(): pl.pallas_call(outputs, name='outputs', grid=(steps,), out_shape=(jax.Sha...]
  transfers between devices with their start and end apart: 3 -> 0, of which waited for: 3 -> 0; matrix products, arithmetic and copies ran while one was open for 8% -> 0% of each run, Pallas kernels for 0% -> 0%
where the time goes in v1:
time: 81.4 us; the launch traced here: 81 us
  Pallas kernels  80.4 us (99%)
    pallas_call x1, Pallas kernels, on_device(): pl.pallas_call(functools.partial(exchange, groups, shards), name='exchang...  71.7 us
    pallas_call x1, Pallas kernels, on_device(): pl.pallas_call(outputs, name='outputs', grid=(steps,), out_shape=(jax.Sha...  8.68 us

profile of v1, /device:TPU:0, one launch (start us, length us, event | category | flops | bytes accessed | tf_op | source)
XLA Modules:
  0.0 81.0 jit_solution(6339318702211982008)
XLA Ops:
  0.6 71.7 %exchange.1 = (bf16[256,64]{1,0:T(8,128)(2,1)}, bf16[256,64]{1,0:T(8,128)(2,1)}, bf16[128,256]{1,0:T(8,128)(2,1)}, f32[128,128]{1,0:T(8,128)}, bf16[8,64,1024]{2...) custom-call(s32[64]{0:T(128)} %bm.1, s32[16]{0:T(128)} %owners.1, ...), custom_call_target="tpu_custom_call" | custom-call | tf_op jit(solution)/shard_map/exchange/pallas_call | solution.py:418
  72.3 8.7 %outputs.1 = (bf16[256,16384]{1,0:T(8,128)(2,1)}, bf16[256,8192]{1,0:T(8,128)(2,1)}, f32[8,16,1024]{2,1,0:T(8,128)}, f32[8,16,2048]{2,1,0:T(8,128)}) custom-call(bf16[256,64]{1,0:T(8,128)(2,1)} %get-tuple-element.11.low, bf16[256,64]{1,0:T(8,128)(2,1)} %get-tuple-element.12.back, bf16[128,256]{1,0:T(8,128)(2,1)} %get-tuple-element.13.pick, ...), custom_call_target="tpu_custom_call" | custom-call | tf_op jit(solution)/shard_map/outputs/pallas_call | solution.py:470

commit v2 on v1

--- a/solution.py
+++ b/solution.py
@@ -82,11 +82,6 @@
             cotangent.at[:, pl.ds(pl.multiple_of(s * 2 * wp, 128), 2 * wp)], cot.at[s], cot_sem.at[s]
         )
 
-    for s in range(shards):
-        load_tok(s).start()
-    for s in range(shards):
-        load_cot(s).start()
-
     used = used_adapters(bm, g * group_blocks, group_blocks, adapters - 1)
 
     def weights(piece, shard):
@@ -290,11 +285,20 @@
         maps[1 + half][f] = jnp.concatenate(
             [b_f32[u, :, half * wp:(half + 1) * wp].astype(BF16) for u in used], axis=0
         )
+    @pl.when(at_end)
+    def _():
+        gather_own(1)
+        gather_own(2)
+
+    for s in range(shards):
+        load_tok(s).start()
+    for s in range(shards):
+        load_cot(s).start()
     acc[...] = jnp.zeros_like(acc)
     gather_span(0, 0, 2)
-    gather_own(1)
+    pl.when(jnp.logical_not(at_end))(lambda: gather_own(1))
     gather_span(0, 2, 4 * line)
-    gather_own(2)
+    pl.when(jnp.logical_not(at_end))(lambda: gather_own(2))
     for s in range(shards):
         load_tok(s).wait()
     accumulate(0)
@@ -308,15 +312,20 @@
 
     acc[...] = jnp.zeros_like(acc)
     gather_span(1, 0, 4 * line)
-    accumulate(1)
+    pl.when(at_end)(lambda: accumulate(1))
     gather_span(2, 0, 4 * line)
+
+    @pl.when(jnp.logical_not(at_end))
+    def _():
+        pass_on((0, 1))
+        accumulate(1)
+
     accumulate(2)
     back = masked(acc[...])
     back_out[...] = back.astype(BF16)
     left_t[...] = back.T.astype(BF16)
     partials((2,), tok)
     pl.when(at_end)(lambda: pass_on((2,)))
-    pl.when(jnp.logical_not(at_end))(lambda: pass_on((0, 1)))
 
     store_d = pltpu.make_async_copy(wd, wd_out, store_sem.at[0])
     store_l = pltpu.make_async_copy(wu_low, wu_out.at[0], store_sem.at[1])

time: 81.4 us -> 75.3 us (0.925)
  Pallas kernels: 80.4 us -> 74.4 us
    pallas_call x1, Pallas kernels: 71.7 us -> 65.7 us  [on_device(): pl.pallas_call(functools.partial(exchange, groups, shards), name='exchang...]
where the time goes in v2:
time: 75.3 us; the launch traced here: 75.1 us
  Pallas kernels  74.4 us (99%)
    pallas_call x1, Pallas kernels, on_device(): pl.pallas_call(functools.partial(exchange, groups, shards), name='exchang...  65.7 us
    pallas_call x1, Pallas kernels, on_device(): pl.pallas_call(outputs, name='outputs', grid=(steps,), out_shape=(jax.Sha...  8.68 us

profile of v2, /device:TPU:0, one launch (start us, length us, event | category | flops | bytes accessed | tf_op | source)
XLA Modules:
  0.0 75.1 jit_solution(7505516179769566917)
XLA Ops:
  0.6 65.7 %exchange.1 = (bf16[256,64]{1,0:T(8,128)(2,1)}, bf16[256,64]{1,0:T(8,128)(2,1)}, bf16[128,256]{1,0:T(8,128)(2,1)}, f32[128,128]{1,0:T(8,128)}, bf16[8,64,1024]{2...) custom-call(s32[64]{0:T(128)} %bm.1, s32[16]{0:T(128)} %owners.1, ...), custom_call_target="tpu_custom_call" | custom-call | tf_op jit(solution)/shard_map/exchange/pallas_call | solution.py:427
  66.4 8.7 %outputs.1 = (bf16[256,16384]{1,0:T(8,128)(2,1)}, bf16[256,8192]{1,0:T(8,128)(2,1)}, f32[8,16,1024]{2,1,0:T(8,128)}, f32[8,16,2048]{2,1,0:T(8,128)}) custom-call(bf16[256,64]{1,0:T(8,128)(2,1)} %get-tuple-element.11.low, bf16[256,64]{1,0:T(8,128)(2,1)} %get-tuple-element.12.back, bf16[128,256]{1,0:T(8,128)(2,1)} %get-tuple-element.13.pick, ...), custom_call_target="tpu_custom_call" | custom-call | tf_op jit(solution)/shard_map/outputs/pallas_call | solution.py:479

commit v3 on v2

--- a/solution.py
+++ b/solution.py
@@ -183,22 +183,20 @@
             device_id=(g, mate), device_id_type=MESH,
         )
 
-    def partials(pieces, values):
-        for i, (side, dist) in enumerate(steps):
-            d = z + side * dist
-
-            @pl.when(here((side, dist)))
-            def _():
-                given = jnp.dot(
-                    left_t[...], values[d * 2 + (1 - c)], preferred_element_type=F32
-                )
-                for n, p in enumerate(pieces):
-                    to_mate[p, i] = given[:, n * wp:(n + 1) * wp].astype(BF16)
-                for p in pieces:
-                    mate_copy(p, i).start()
-                kept = jnp.dot(left_t[...], values[d * 2 + c], preferred_element_type=F32)
-                for n, p in enumerate(pieces):
-                    own_part[p, i] = kept[:, n * wp:(n + 1) * wp]
+    def partial_step(pieces, values, i):
+        side, dist = steps[i]
+        d = z + side * dist
+
+        @pl.when(here((side, dist)))
+        def _():
+            given = jnp.dot(left_t[...], values[d * 2 + (1 - c)], preferred_element_type=F32)
+            for n, p in enumerate(pieces):
+                to_mate[p, i] = given[:, n * wp:(n + 1) * wp].astype(BF16)
+            for p in pieces:
+                mate_copy(p, i).start()
+            kept = jnp.dot(left_t[...], values[d * 2 + c], preferred_element_type=F32)
+            for n, p in enumerate(pieces):
+                own_part[p, i] = kept[:, n * wp:(n + 1) * wp]
 
     def run_copy(p, side, dist):
         row = (1 - side) // 2
@@ -212,47 +210,73 @@
         run_copy(p, side, dist + 1).wait_recv()
         return arrived[p, (1 - side) // 2, dist].astype(F32)
 
-    def pass_on(pieces):
-        for i, (side, dist) in enumerate(steps[:-1]):
-            fed = has_left if side > 0 else has_right
-
-            @pl.when(here((side, dist)))
-            def _():
-                for p in pieces:
-                    mate_copy(p, i).wait_recv()
-                    if dist < line - 1:
-                        @pl.when(fed)
-                        def _():
-                            running[p, i] = (
-                                own_part[p, i]
-                                + from_mate[p, i].astype(F32)
-                                + run_wait(p, side, dist)
-                            ).astype(BF16)
-
-                        @pl.when(jnp.logical_not(fed))
-                        def _():
-                            running[p, i] = (
-                                own_part[p, i] + from_mate[p, i].astype(F32)
-                            ).astype(BF16)
-                    else:
+    def pass_step(pieces, i):
+        side, dist = steps[i]
+        fed = has_left if side > 0 else has_right
+
+        @pl.when(here((side, dist)))
+        def _():
+            for p in pieces:
+                mate_copy(p, i).wait_recv()
+                if dist < line - 1:
+                    @pl.when(fed)
+                    def _():
+                        running[p, i] = (
+                            own_part[p, i]
+                            + from_mate[p, i].astype(F32)
+                            + run_wait(p, side, dist)
+                        ).astype(BF16)
+
+                    @pl.when(jnp.logical_not(fed))
+                    def _():
                         running[p, i] = (own_part[p, i] + from_mate[p, i].astype(F32)).astype(
                             BF16
                         )
-                    run_copy(p, side, dist).start()
-
-    def grp_copy(p, step):
+                else:
+                    running[p, i] = (own_part[p, i] + from_mate[p, i].astype(F32)).astype(BF16)
+                run_copy(p, side, dist).start()
+
+    def pass_on(pieces):
+        for i in range(last):
+            pass_step(pieces, i)
+
+    def partials(pieces, values):
+        for i in range(len(steps)):
+            partial_step(pieces, values, i)
+            if i >= 2:
+                pl.when(at_end)(lambda: pass_step(pieces, i - 2))
+        pl.when(at_end)(lambda: pass_step(pieces, last - 1))
+
+    beside, across = g + 1 - 2 * (g % 2), (g + 2) % groups
+
+    def half_of(ref, half):
+        return ref.at[pl.ds(half * (ROWS // 2), ROWS // 2)]
+
+    def grp_copy(p, n):
+        near, half, far = ((beside, 0, g), (beside, 1, g), (across, 0, g), (across, 1, g),
+                           (across, 0, beside), (beside, 1, across))[n]
+        place = half_of(shares_out.at[p, far], half)
         return pltpu.make_async_remote_copy(
-            src_ref=final.at[p], dst_ref=shares_out.at[p, g],
-            send_sem=grp_send.at[p, step], recv_sem=grp_recv.at[p, g],
-            device_id=((g + step) % groups, f), device_id_type=MESH,
-        )
-
-    def grp_wait(p, other):
+            src_ref=half_of(final.at[p], half) if n < 4 else place, dst_ref=place,
+            send_sem=grp_send.at[p, n], recv_sem=grp_recv.at[p, n],
+            device_id=(near, f), device_id_type=MESH,
+        )
+
+    def grp_wait(p, n):
+        far, half = ((beside, 0), (beside, 1), (across, 0), (across, 1),
+                     (groups - 1 - g, 0), (groups - 1 - g, 1))[n]
+        place = half_of(shares_out.at[p, far], half)
         pltpu.make_async_remote_copy(
-            src_ref=final.at[p], dst_ref=shares_out.at[p, other],
-            send_sem=grp_send.at[p, 0], recv_sem=grp_recv.at[p, other],
-            device_id=(g, mate), device_id_type=MESH,
+            src_ref=place, dst_ref=place,
+            send_sem=grp_send.at[p, n], recv_sem=grp_recv.at[p, n],
+            device_id=(beside, f), device_id_type=MESH,
         ).wait_recv()
+
+    def relay(p):
+        grp_wait(p, 0)
+        grp_copy(p, 4).start()
+        grp_wait(p, 3)
+        grp_copy(p, 5).start()
 
     def keep_copy(p):
         return pltpu.make_async_copy(final.at[p], shares_out.at[p, g], keep_sem.at[p])
@@ -270,8 +294,8 @@
             own_part[p, last] += run_wait(p, -1, 0)
 
         final[p] = own_part[p, last].astype(BF16)
-        for step in range(1, groups):
-            grp_copy(p, step).start()
+        for n in (0, 3, 1, 2):
+            grp_copy(p, n).start()
         keep_copy(p).start()
 
     load_a.wait()
@@ -308,7 +332,6 @@
     for s in range(shards):
         load_cot(s).wait()
     partials((0, 1), cot)
-    pl.when(at_end)(lambda: pass_on((0, 1)))
 
     acc[...] = jnp.zeros_like(acc)
     gather_span(1, 0, 4 * line)
@@ -325,7 +348,6 @@
     back_out[...] = back.astype(BF16)
     left_t[...] = back.T.astype(BF16)
     partials((2,), tok)
-    pl.when(at_end)(lambda: pass_on((2,)))
 
     store_d = pltpu.make_async_copy(wd, wd_out, store_sem.at[0])
     store_l = pltpu.make_async_copy(wu_low, wu_out.at[0], store_sem.at[1])
@@ -336,6 +358,7 @@
 
     finish_piece(0)
     finish_piece(1)
+    relay(0)
     pl.when(jnp.logical_not(at_end))(lambda: pass_on((2,)))
 
     names = [
@@ -372,7 +395,9 @@
         uses = jnp.where(wide == k, totals[k], uses)
     scale_out[...] = 1.0 / (BLOCK * jnp.maximum(uses, 1)).astype(F32)
 
+    relay(1)
     finish_piece(2)
+    relay(2)
     for piece in range(PIECES):
         gather_finish(piece)
 
@@ -389,10 +414,10 @@
     store_h.wait()
     for p in range(PIECES):
         keep_copy(p).wait()
-        for step in range(1, groups):
-            grp_copy(p, step).wait_send()
-        for step in range(1, groups):
-            grp_wait(p, (g + step) % groups)
+        for n in range(6):
+            grp_copy(p, n).wait_send()
+        for n in (1, 2, 4, 5):
+            grp_wait(p, n)
 
 
 def outputs(
@@ -420,6 +445,7 @@
     wp = adapter_a.shape[2]
     assert adapter_b.shape[2] == 2 * wp
     line = shards // 2
+    assert groups == 4
     dma = pltpu.SemaphoreType.DMA
     vmem = pl.BlockSpec(memory_space=pltpu.VMEM)
     smem = pl.BlockSpec(memory_space=pltpu.SMEM)
@@ -464,8 +490,8 @@
             dma((PIECES, 2 * line - 1)),
             dma((PIECES, 2 * line - 1)),
             dma((PIECES, 2, line)),
-            dma((PIECES, groups)),
-            dma((PIECES, groups)),
+            dma((PIECES, 6)),
+            dma((PIECES, 6)),
             dma((PIECES,)),
         ],
         compiler_params=pltpu.CompilerParams(

time: 75.3 us -> 76.1 us (1.011)
  Pallas kernels: 74.4 us -> 75.2 us
    pallas_call x1, Pallas kernels: 65.7 us -> 66.5 us  [on_device(): pl.pallas_call(functools.partial(exchange, groups, shards), name='exchang...]
where the time goes in v3:
time: 76.1 us; the launch traced here: 75.9 us
  Pallas kernels  75.2 us (99%)
    pallas_call x1, Pallas kernels, on_device(): pl.pallas_call(functools.partial(exchange, groups, shards), name='exchang...  66.5 us
    pallas_call x1, Pallas kernels, on_device(): pl.pallas_call(outputs, name='outputs', grid=(steps,), out_shape=(jax.Sha...  8.68 us

profile of v3, /device:TPU:0, one launch (start us, length us, event | category | flops | bytes accessed | tf_op | source)
XLA Modules:
  0.0 75.9 jit_solution(8854131951872733155)
XLA Ops:
  0.6 66.5 %exchange.1 = (bf16[256,64]{1,0:T(8,128)(2,1)}, bf16[256,64]{1,0:T(8,128)(2,1)}, bf16[128,256]{1,0:T(8,128)(2,1)}, f32[128,128]{1,0:T(8,128)}, bf16[8,64,1024]{2...) custom-call(s32[64]{0:T(128)} %bm.1, s32[16]{0:T(128)} %owners.1, ...), custom_call_target="tpu_custom_call" | custom-call | tf_op jit(solution)/shard_map/exchange/pallas_call | solution.py:453
  67.2 8.7 %outputs.1 = (bf16[256,16384]{1,0:T(8,128)(2,1)}, bf16[256,8192]{1,0:T(8,128)(2,1)}, f32[8,16,1024]{2,1,0:T(8,128)}, f32[8,16,2048]{2,1,0:T(8,128)}) custom-call(bf16[256,64]{1,0:T(8,128)(2,1)} %get-tuple-element.11.low, bf16[256,64]{1,0:T(8,128)(2,1)} %get-tuple-element.12.back, bf16[128,256]{1,0:T(8,128)(2,1)} %get-tuple-element.13.pick, ...), custom_call_target="tpu_custom_call" | custom-call | tf_op jit(solution)/shard_map/outputs/pallas_call | solution.py:505

commit v4 on v3

--- a/solution.py
+++ b/solution.py
@@ -247,36 +247,19 @@
                 pl.when(at_end)(lambda: pass_step(pieces, i - 2))
         pl.when(at_end)(lambda: pass_step(pieces, last - 1))
 
-    beside, across = g + 1 - 2 * (g % 2), (g + 2) % groups
-
-    def half_of(ref, half):
-        return ref.at[pl.ds(half * (ROWS // 2), ROWS // 2)]
-
-    def grp_copy(p, n):
-        near, half, far = ((beside, 0, g), (beside, 1, g), (across, 0, g), (across, 1, g),
-                           (across, 0, beside), (beside, 1, across))[n]
-        place = half_of(shares_out.at[p, far], half)
+    def grp_copy(p, step):
         return pltpu.make_async_remote_copy(
-            src_ref=half_of(final.at[p], half) if n < 4 else place, dst_ref=place,
-            send_sem=grp_send.at[p, n], recv_sem=grp_recv.at[p, n],
-            device_id=(near, f), device_id_type=MESH,
-        )
-
-    def grp_wait(p, n):
-        far, half = ((beside, 0), (beside, 1), (across, 0), (across, 1),
-                     (groups - 1 - g, 0), (groups - 1 - g, 1))[n]
-        place = half_of(shares_out.at[p, far], half)
+            src_ref=final.at[p], dst_ref=shares_out.at[p, g],
+            send_sem=grp_send.at[p, step], recv_sem=grp_recv.at[p, g],
+            device_id=((g + step) % groups, f), device_id_type=MESH,
+        )
+
+    def grp_wait(p, other):
         pltpu.make_async_remote_copy(
-            src_ref=place, dst_ref=place,
-            send_sem=grp_send.at[p, n], recv_sem=grp_recv.at[p, n],
-            device_id=(beside, f), device_id_type=MESH,
+            src_ref=final.at[p], dst_ref=shares_out.at[p, other],
+            send_sem=grp_send.at[p, 0], recv_sem=grp_recv.at[p, other],
+            device_id=(g, mate), device_id_type=MESH,
         ).wait_recv()
-
-    def relay(p):
-        grp_wait(p, 0)
-        grp_copy(p, 4).start()
-        grp_wait(p, 3)
-        grp_copy(p, 5).start()
 
     def keep_copy(p):
         return pltpu.make_async_copy(final.at[p], shares_out.at[p, g], keep_sem.at[p])
@@ -294,8 +277,8 @@
             own_part[p, last] += run_wait(p, -1, 0)
 
         final[p] = own_part[p, last].astype(BF16)
-        for n in (0, 3, 1, 2):
-            grp_copy(p, n).start()
+        for step in range(1, groups):
+            grp_copy(p, step).start()
         keep_copy(p).start()
 
     load_a.wait()
@@ -358,7 +341,6 @@
 
     finish_piece(0)
     finish_piece(1)
-    relay(0)
     pl.when(jnp.logical_not(at_end))(lambda: pass_on((2,)))
 
     names = [
@@ -395,9 +377,7 @@
         uses = jnp.where(wide == k, totals[k], uses)
     scale_out[...] = 1.0 / (BLOCK * jnp.maximum(uses, 1)).astype(F32)
 
-    relay(1)
     finish_piece(2)
-    relay(2)
     for piece in range(PIECES):
         gather_finish(piece)
 
@@ -414,10 +394,10 @@
     store_h.wait()
     for p in range(PIECES):
         keep_copy(p).wait()
-        for n in range(6):
-            grp_copy(p, n).wait_send()
-        for n in (1, 2, 4, 5):
-            grp_wait(p, n)
+        for step in range(1, groups):
+            grp_copy(p, step).wait_send()
+        for step in range(1, groups):
+            grp_wait(p, (g + step) % groups)
 
 
 def outputs(
@@ -445,7 +425,6 @@
     wp = adapter_a.shape[2]
     assert adapter_b.shape[2] == 2 * wp
     line = shards // 2
-    assert groups == 4
     dma = pltpu.SemaphoreType.DMA
     vmem = pl.BlockSpec(memory_space=pltpu.VMEM)
     smem = pl.BlockSpec(memory_space=pltpu.SMEM)
@@ -490,8 +469,8 @@
             dma((PIECES, 2 * line - 1)),
             dma((PIECES, 2 * line - 1)),
             dma((PIECES, 2, line)),
-            dma((PIECES, 6)),
-            dma((PIECES, 6)),
+            dma((PIECES, groups)),
+            dma((PIECES, groups)),
             dma((PIECES,)),
         ],
         compiler_params=pltpu.CompilerParams(

time: 76.1 us -> 73.2 us (0.962)
  the two profiles are of different devices: /device:TPU:0 before, /device:TPU:12 now
where the time goes in v4:
time: 73.2 us; the launch traced here: 73 us
  Pallas kernels  72.3 us (99%)
    pallas_call x1, Pallas kernels, on_device(): pl.pallas_call(functools.partial(exchange, groups, shards), name='exchang...  63.6 us
    pallas_call x1, Pallas kernels, on_device(): pl.pallas_call(outputs, name='outputs', grid=(steps,), out_shape=(jax.Sha...  8.69 us

profile of v4, /device:TPU:12, one launch (start us, length us, event | category | flops | bytes accessed | tf_op | source)
XLA Modules:
  0.0 73.0 jit_solution(17876444888010630815)
XLA Ops:
  0.6 63.6 %exchange.1 = (bf16[256,64]{1,0:T(8,128)(2,1)}, bf16[256,64]{1,0:T(8,128)(2,1)}, bf16[128,256]{1,0:T(8,128)(2,1)}, f32[128,128]{1,0:T(8,128)}, bf16[8,64,1024]{2...) custom-call(s32[64]{0:T(128)} %bm.1, s32[16]{0:T(128)} %owners.1, ...), custom_call_target="tpu_custom_call" | custom-call | tf_op jit(solution)/shard_map/exchange/pallas_call | solution.py:432
  64.3 8.7 %outputs.1 = (bf16[256,16384]{1,0:T(8,128)(2,1)}, bf16[256,8192]{1,0:T(8,128)(2,1)}, f32[8,16,1024]{2,1,0:T(8,128)}, f32[8,16,2048]{2,1,0:T(8,128)}) custom-call(bf16[256,64]{1,0:T(8,128)(2,1)} %get-tuple-element.11.low, bf16[256,64]{1,0:T(8,128)(2,1)} %get-tuple-element.12.back, bf16[128,256]{1,0:T(8,128)(2,1)} %get-tuple-element.13.pick, ...), custom_call_target="tpu_custom_call" | custom-call | tf_op jit(solution)/shard_map/outputs/pallas_call | solution.py:484
